TPU v7x, 32 devices: a whole 2x2x4 slice. The times are simulated.
32 devices in a mesh: seq: 8 (over z, x), vocab: 4 (over y, core).
Axes of the slice: x: 2, y: 2, z: 4, core: 2. Of those that a mesh axis runs over, the one named last changes fastest.
Arguments:
- hidden: bfloat16 [2, 1024, 2048], P(None, 'seq'), may hold values from -6 to 6
- embedded: bfloat16 [2, 1024, 2048], P(None, 'seq'), may hold values from -6 to 6
- targets: int32 [2, 1024], P(None, 'seq'), may hold values from 0 to 51199
- main_mask: int32 [2, 1024], P(None, 'seq'), may hold values 0 or 1
- mtp_mask: int32 [2, 1024], P(None, 'seq'), may hold values from 0 to 1, as said below
- lengths: int32 [2], replicated, may hold values from 256 to 1024, as said below
- head_weight: bfloat16 [2048, 51200], P(None, ('seq', 'vocab')), may hold values from -7.6733202 to 7.6733202
- projection: bfloat16 [4096, 2048], P(None, 'vocab'), may hold values from -0.09375 to 0.09375
- main_gain: float32 [2048], replicated, may hold values from 0.5 to 1.5
- hidden_gain: float32 [2048], replicated, may hold values from 0.5 to 1.5
- embed_gain: float32 [2048], replicated, may hold values from 0.5 to 1.5
- mtp_gain: float32 [2048], replicated, may hold values from 0.5 to 1.5
Outputs:
- main_tokens: float32 [2, 1024], P(None, 'seq')
- mtp_tokens: float32 [2, 1024], P(None, 'seq')
- total_loss: float32 [], replicated
Inputs may be any that keep to these rules, and one draw needn't show every extreme that they name: `mtp_mask`: 1 at every position that is a multiple of 128. `lengths`: the first sequence has length 1024.
All inputs are finite; a program needn't handle non-finite values. No bound on the sum of `main_mask` on one device may be relied on, other than what follows from the above.
Results may differ from a plain program's by a relative error of at most 0.0004.
The roundings to bfloat16 on the way count: a program that leaves them out, or rounds other values in their place, can miss the bound.
Values may be sent and summed in bfloat16 or wider, within the bound.
A program may use at most 128 MiB of HBM per device.

v0:
```python
import jax
import jax.numpy as jnp
from jax import lax
from jax.sharding import PartitionSpec as P

EPSILON = 1e-06
MTP_WEIGHT = 0.3


def from_behind(block, axis, distance):
    devices = range(lax.axis_size(axis))
    route = [(i - distance, i) for i in devices if i - distance in devices]
    return lax.ppermute(block, axis, route)


def partner_2(value, axis, apart):
    mask = 2**apart
    pairs = [(source, source ^ mask) for source in range(lax.axis_size(axis))]
    return lax.ppermute(value, axis, pairs)


def normalize(values, gain_vec):
    values = values.astype(jnp.float32)
    mean_square = jnp.mean(values * values, axis=-1, keepdims=True)
    return values * lax.rsqrt(mean_square + EPSILON) * gain_vec


def column_stats(logits, column_ids, wanted):
    highest = jnp.max(logits, axis=1)
    exp_total = jnp.sum(jnp.exp(logits - highest[:, None]), axis=1)
    picked = jnp.sum(jnp.where(column_ids[None, :] == wanted[:, None], logits, 0.0), axis=1)
    return (highest, exp_total, picked)


def join_stats(earlier, latter):
    highest = jnp.maximum(earlier[0], latter[0])
    exp_total = earlier[1] * jnp.exp(earlier[0] - highest) + latter[1] * jnp.exp(
        latter[0] - highest
    )
    return (highest, exp_total, earlier[2] + latter[2])


def shards(
    hidden,
    embedded,
    targets,
    main_mask,
    mtp_mask,
    lengths,
    head_weight,
    projection,
    main_gain,
    hidden_gain,
    embed_gain,
    mtp_gain,
):
    batches, seq_len, model_width = hidden.shape
    seq_index = lax.axis_index("seq")
    vocab_index = lax.axis_index("vocab")
    vocab_count = lax.axis_size("vocab")
    block_cols = head_weight.shape[1]
    positions = seq_index * seq_len + lax.broadcasted_iota(jnp.int32, (batches, seq_len), 1)
    length_col = lengths[:, None]
    keep_main = ((main_mask == 1) & (positions + 1 < length_col)).astype(jnp.float32)
    keep_mtp = ((mtp_mask == 1) & (positions >= 1) & (positions + 1 < length_col)).astype(
        jnp.float32
    )
    count_main = jnp.sum(keep_main)
    count_mtp = jnp.sum(keep_mtp)
    counted = lax.psum((count_main, count_mtp), "seq")
    main_rows = normalize(hidden, main_gain).astype(jnp.bfloat16).reshape(-1, model_width)
    incoming = from_behind(hidden[:, seq_len - 1 :, :], "seq", 1)
    previous = jnp.concatenate([incoming, hidden[:, : seq_len - 1, :]], axis=1)
    joined = jnp.concatenate(
        [normalize(previous, hidden_gain), normalize(embedded, embed_gain)], axis=2
    )
    joined = joined.astype(jnp.bfloat16).reshape(-1, 2 * model_width)
    partial_value = jnp.dot(joined, projection, preferred_element_type=jnp.float32).astype(
        jnp.bfloat16
    )
    mixed = lax.all_gather(partial_value, "vocab", axis=1, tiled=True)
    mtp_rows = normalize(mixed, mtp_gain).astype(jnp.bfloat16)
    all_rows = jnp.concatenate([main_rows, mtp_rows], axis=0)
    flat_targets = targets.reshape(-1)
    wanted = jnp.concatenate([flat_targets, flat_targets], axis=0)
    held_cols = head_weight
    levels = lax.axis_size("seq").bit_length() - 1
    for bit_number in range(1, levels):
        received = partner_2(held_cols, "seq", bit_number)
        upper_half = seq_index >> bit_number & 1 == 1
        held_cols = jnp.where(
            upper_half,
            jnp.concatenate([received, held_cols], axis=1),
            jnp.concatenate([held_cols, received], axis=1),
        )
    partner = partner_2(all_rows, "seq", 0)
    partner_wanted = partner_2(wanted, "seq", 0)
    column_pos = lax.broadcasted_iota(jnp.int32, (held_cols.shape[1],), 0)
    anchor_seq = (seq_index & 1) + 2 * (column_pos // block_cols)
    column_ids = (anchor_seq * vocab_count + vocab_index) * block_cols + column_pos % block_cols
    logits = jnp.dot(
        jnp.concatenate([all_rows, partner], axis=0), held_cols, preferred_element_type=jnp.float32
    )
    row_count = all_rows.shape[0]
    own_stats = column_stats(logits[:row_count], column_ids, wanted)
    peer_stats = column_stats(logits[row_count:], column_ids, partner_wanted)
    returned = partner_2((peer_stats[0], peer_stats[1], peer_stats[2]), "seq", 0)
    highest, exp_total, picked = join_stats(own_stats, returned)
    global_max = lax.pmax(highest, "vocab")
    global_total, target_logit = lax.psum(
        (exp_total * jnp.exp(highest - global_max), picked), "vocab"
    )
    losses = global_max + jnp.log(global_total) - target_logit
    half_rows = batches * seq_len
    main_tokens = keep_main * losses[:half_rows].reshape(batches, seq_len)
    mtp_tokens = keep_mtp * losses[half_rows:].reshape(batches, seq_len)
    main_sum = jnp.sum(main_tokens)
    mtp_sum = jnp.sum(mtp_tokens)
    summed = lax.psum((main_sum, mtp_sum), "seq")
    total_main, total_mtp = summed
    kept_main, kept_mtp = counted
    total_loss = total_main / jnp.maximum(kept_main, 1.0) + MTP_WEIGHT * total_mtp / jnp.maximum(
        kept_mtp, 1.0
    )
    return (main_tokens, mtp_tokens, total_loss)


def solution(mesh):
    return jax.shard_map(
        shards,
        mesh=mesh,
        in_specs=(
            P(None, "seq", None),
            P(None, "seq", None),
            P(None, "seq"),
            P(None, "seq"),
            P(None, "seq"),
            P(),
            P(None, ("seq", "vocab")),
            P(None, "vocab"),
            P(),
            P(),
            P(),
            P(),
        ),
        out_specs=(P(None, "seq"), P(None, "seq"), P()),
        check_vma=False,
    )
```

profile of v0, /device:TPU:0, one launch (start us, length us, event | category | flops | bytes accessed | tf_op | source)
XLA Modules:
  0.0 926.5 jit_solution(852602479931637078)
XLA Ops:
  7.2 0.0 all-gather.2.cloned.1.call-start
  7.2 3.1 collective-permute-start.2
  10.3 0.0 copy-start.1
  10.3 0.0 copy-start.2
  10.3 0.0 copy-start.3
  10.3 141.4 %collective-permute-done.2 = bf16[2048,1600]{0,1:T(8,128)(2,1)} collective-permute-done((bf16[2048,1600]{0,1:T(8,128)(2,1)}, bf16[2048,1600]{0,1:T(8,128)(2,1)}, u32[]{:S(2)}, u32[]{:S(2)}) %collective-permute-start.2) | collective-permute-done | bytes 6553632 | tf_op jit(solution)/shard_map/ppermute | solution.py:19
  151.8 15.6 %maximum_select_fusion.2 = bf16[2048,3200]{0,1:T(8,128)(2,1)} fusion(bf16[2048,1600]{0,1:T(8,128)(2,1)} %param.18, bf16[2048,1600]{0,1:T(8,128)(2,1)} %collective-permute-done.2, pred[]{:T(512)S(6)} %eq.40), kind=kLoop, calls=%fused_computation.8 | loop fusion | flops 58982400 | bytes 26214400 | tf_op jit(solution)/shard_map/jit(_where)/select_n | solution.py:91
  167.4 0.0 copy-start.4
  167.4 0.0 copy-start.11
  167.4 2.8 collective-permute-start.3
  170.2 0.0 copy-done.1
  170.2 3.4 collective-permute-start
  173.7 0.0 copy-done.2
  173.7 0.3 fusion.15
  174.0 0.0 copy-done.3
  174.0 0.3 fusion.17
  174.3 0.8 collective-permute-done
  175.1 0.4 multiply_reduce_fusion
  175.5 0.3 maximum_convert_fusion
  175.8 0.0 copy-done.4
  175.9 0.0 copy-start.5
  175.9 0.2 fusion.26
  176.1 0.0 copy-done.11
  176.1 0.0 copy-start.6
  176.1 2.0 fusion.27
  178.1 0.0 copy-start.7
  178.1 0.0 all-gather.2.cloned.1.call-update
  178.1 0.3 fusion.12
  178.4 0.0 copy-done.5
  178.4 0.3 fusion.14
  178.8 573.8 %all-gather.2.cloned.1.call-done = bf16[256,2048]{1,0:T(8,128)(2,1)} async-done(((bf16[256,512]{1,0:T(8,128)(2,1)}), bf16[256,2048]{1,0:T(8,128)(2,1)}) %all-gather.2.cloned.1.call-update) | async-done | bytes 1048592 | tf_op jit(solution)/shard_map/all_gather | solution.py:81
  752.6 1.5 fusion.18
  754.1 0.0 copy-done.6
  754.1 1.5 fusion.20
  755.6 1.5 pad_maximum_fusion
  757.1 1.5 collective-permute-start.1
  758.6 0.0 copy-done.7
  758.6 0.6 collective-permute-start.6
  759.3 45.9 %collective-permute-done.1 = bf16[512,2048]{1,0:T(8,128)(2,1)} collective-permute-done((bf16[512,2048]{1,0:T(8,128)(2,1)}, bf16[512,2048]{1,0:T(8,128)(2,1)}, u32[]{:S(2)}, u32[]{:S(2)}) %collective-permute-start.1) | collective-permute-done | bytes 2097184 | tf_op jit(solution)/shard_map/ppermute | solution.py:19
  805.2 0.0 collective-permute-done.3
  805.2 49.2 %fusion = f32[1024,6400]{1,0:T(8,128)} fusion(bf16[2048,3200]{0,1:T(8,128)(2,1)} %maximum_select_fusion.2, bf16[2048,3200]{0,1:T(8,128)(2,1)} %collective-permute-done.3, pred[]{:T(512)S(6)} %eq.39, bf16[512,2048]{1,0:T(8,128)(2,1)} %collective-permute-done.1, bf16[256,2048]{1,0:T(8,128)(2,1)S(1)} %fusion.20, bf16[256,2048]{1,0:T(8,128)(2,1)S(1)} %bitcast.22), kind=kOutput, calls=%fused_computation.1 | convolution fusion | flops 26974093312 | bytes 56623104 | tf_op jit(solution)/shard_map/dot_general | solution.py:101
  854.4 0.0 copy-start
  854.4 9.4 %slice_reduce_fusion = (f32[512]{0:T(512)S(1)}, f32[512]{0:T(512)S(1)}) fusion(f32[1024,6400]{1,0:T(8,128)} %fusion), kind=kLoop, calls=%fused_computation.13 | loop fusion | flops 6552576 | bytes 26218496 | tf_op jit(solution)/shard_map/reduce_max | solution.py:29
  863.8 1.5 collective-permute-start.4
  865.4 0.0 collective-permute-done.6
  865.4 5.0 copy-done
  870.4 0.0 copy-start.8
  870.4 0.0 copy-start.9
  870.4 0.0 copy-start.10
  870.4 6.9 exponential_reduce_fusion.1
  877.3 1.5 collective-permute-start.7
  878.8 0.0 copy-done.8
  878.9 0.0 copy-done.9
  878.9 0.0 copy-done.10
  878.9 0.8 convert_reduce_fusion
  879.6 0.6 collective-permute-start.5
  880.2 0.0 collective-permute-done.4
  880.2 0.8 collective-permute-done.7
  881.0 5.7 pmax.7
  886.7 0.0 collective-permute-done.5
  886.7 5.8 all-reduce.1
  892.5 1.2 fusion.47
  893.7 22.3 %all-reduce = (f32[]{:T(128)}, f32[]{:T(128)}, f32[]{:T(128)}, f32[]{:T(128)}) all-reduce(f32[]{:T(128)} %get-tuple-element.25, f32[]{:T(128)} %get-tuple-element.27, f32[]{:T(128)} %get-tuple-element.19, f32[]{:T(128)} %get-tuple-element.17), channel_id=1, replica_groups=mesh['seq'=8,'vocab'=4] {'seq'}, use_global_device_ids=true, to_apply=%region_14.15 | all-reduce | flops 4 | bytes 32 | tf_op jit(solution)/shard_map/psum | solution.py:119
  (13 shorter events, 0.1 us)
Async XLA Ops:
  7.2 745.4 %all-gather.2.cloned.1.call-start = ((), (), s32[]{:S(2)}) async-start(), calls=%async_computation | async-start | bytes 1310720 | tf_op jit(solution)/shard_map/all_gather | solution.py:81
  7.2 144.6 %collective-permute-start.2 = (bf16[2048,1600]{0,1:T(8,128)(2,1)}, bf16[2048,1600]{0,1:T(8,128)(2,1)}, u32[]{:S(2)}, u32[]{:S(2)}) collective-permute-start(bf16[2048,1600]{0,1:T(8,128)(2,1)} %param.18), channel_id=1, source_target_pairs={{0,8},{4,12},{8,0},{12,4},{16,24},{20,28},{24,16},{28,20},{1,9},{5... | collective-permute-start | bytes 19660808 | tf_op jit(solution)/shard_map/ppermute | solution.py:19
  10.3 159.9 %copy-start.1 = (bf16[2,128,2048]{2,1,0:T(8,128)(2,1)S(1)}, bf16[2,128,2048]{2,1,0:T(8,128)(2,1)}, u32[]{:S(2)}) copy-start(bf16[2,128,2048]{2,1,0:T(8,128)(2,1)} %param.12) | copy-start | bytes 3145732
  10.3 163.3 %copy-start.2 = (bf16[2,128,2048]{2,1,0:T(8,128)(2,1)S(1)}, bf16[2,128,2048]{2,1,0:T(8,128)(2,1)}, u32[]{:S(2)}) copy-start(bf16[2,128,2048]{2,1,0:T(8,128)(2,1)} %param.13) | copy-start | bytes 3145732
  10.3 163.6 %copy-start.3 = (f32[2048]{0:T(1024)S(1)}, f32[2048]{0:T(1024)}, u32[]{:S(2)}) copy-start(f32[2048]{0:T(1024)} %param.22) | copy-start | bytes 24580
  167.4 8.4 copy-start.4
  167.4 8.7 copy-start.11
  167.4 637.8 %collective-permute-start.3 = (bf16[2048,3200]{0,1:T(8,128)(2,1)}, bf16[2048,3200]{0,1:T(8,128)(2,1)}, u32[]{:S(2)}, u32[]{:S(2)}) collective-permute-start(bf16[2048,3200]{0,1:T(8,128)(2,1)} %maximum_select_fusion.2), channel_id=1, source_target_pairs={{0,16},{4,20},{8,24},{12,28},{16,0},{20,4},{24,8},{28,12},{1,17},{... | collective-permute-start | bytes 39321608 | tf_op jit(solution)/shard_map/ppermute | solution.py:19
  170.2 4.8 collective-permute-start
  175.9 2.6 copy-start.5
  176.1 578.0 %copy-start.6 = (f32[2048]{0:T(1024)S(1)}, f32[2048]{0:T(1024)}, u32[]{:S(2)}) copy-start(f32[2048]{0:T(1024)} %param.23) | copy-start | bytes 24580
  178.1 580.5 %copy-start.7 = (s32[2,128]{1,0:T(2,128)S(1)}, s32[2,128]{1,0:T(2,128)}, u32[]{:S(2)}) copy-start(s32[2,128]{1,0:T(2,128)} %param.14) | copy-start | bytes 3076
  757.1 48.1 %collective-permute-start.1 = (bf16[512,2048]{1,0:T(8,128)(2,1)}, bf16[512,2048]{1,0:T(8,128)(2,1)}, u32[]{:S(2)}, u32[]{:S(2)}) collective-permute-start(bf16[512,2048]{1,0:T(8,128)(2,1)} %pad_maximum_fusion), channel_id=1, source_target_pairs={{0,4},{4,0},{8,12},{12,8},{16,20},{20,16},{24,28},{28,24},{1,5},{5... | collective-permute-start | bytes 6291464 | tf_op jit(solution)/shard_map/ppermute | solution.py:19
  758.6 106.7 %collective-permute-start.6 = (s32[512]{0:T(512)S(1)}, s32[512]{0:T(512)S(1)}, u32[]{:S(2)}, u32[]{:S(2)}) collective-permute-start(s32[512]{0:T(512)S(1)} %pad_add_fusion), channel_id=1, source_target_pairs={{0,4},{4,0},{8,12},{12,8},{16,20},{20,16},{24,28},{28,24},{1,5},{5... | collective-permute-start | bytes 6152 | tf_op jit(solution)/shard_map/ppermute | solution.py:19
  854.4 16.0 %copy-start = (f32[1024,6400]{1,0:T(8,128)S(1)}, f32[1024,6400]{1,0:T(8,128)}, u32[]{:S(2)}) copy-start(f32[1024,6400]{1,0:T(8,128)} %fusion) | copy-start | bytes 78643200
  863.8 16.3 %collective-permute-start.4 = (f32[512]{0:T(512)S(1)}, f32[512]{0:T(512)S(1)}, u32[]{:S(2)}, u32[]{:S(2)}) collective-permute-start(f32[512]{0:T(512)S(1)} %get-tuple-element.9), channel_id=1, source_target_pairs={{0,4},{4,0},{8,12},{12,8},{16,20},{20,16},{24,28},{28,24},{1,5},{5... | collective-permute-start | bytes 6152 | tf_op jit(solution)/shard_map/ppermute | solution.py:19
  870.4 8.4 copy-start.8
  870.4 8.4 copy-start.9
  870.4 8.4 copy-start.10
  877.3 3.6 collective-permute-start.7
  879.6 7.1 collective-permute-start.5
Sparse Core Ops, SparseCore 0:
  178.3 574.2 all-gather.1
where the time goes:
time: 927 us; the launch traced here: 926 us
  waiting for transfers between devices  763 us (82%)
  matrix products  51.1 us (6%)
  other arithmetic  40.7 us (4%)
  blocking collectives  33.8 us (4%)
  between operations  17.9 us (2%)
  starting transfers between devices  15.1 us (2%)
    all_gather x1, waiting for transfers between devices, shards(): mixed = lax.all_gather(partial_value, 'vocab', axis=1, tiled=True)  574 us
    ppermute x7, waiting for transfers between devices, partner_2(): return lax.ppermute(value, axis, pairs)  188 us
    dot_general x1, matrix products, shards(): jnp.dot(jnp.concatenate([all_rows, partner], axis=0), held_cols, preferre...  49.2 us
    psum x1, blocking collectives, shards(): summed = lax.psum((main_sum, mtp_sum), 'seq')  22.3 us
  transfers between devices with their start and end apart: 9, of which 5 were waited for; matrix products, arithmetic and copies ran while one was open for 8% of the time, Pallas kernels for 0%

commit v1 on v0

--- a/solution.py
+++ b/solution.py
@@ -78,7 +78,14 @@
     partial_value = jnp.dot(joined, projection, preferred_element_type=jnp.float32).astype(
         jnp.bfloat16
     )
-    mixed = lax.all_gather(partial_value, "vocab", axis=1, tiled=True)
+    ring = [partial_value]
+    for hop in range(3):
+        ring.append(lax.ppermute(ring[-1], "vocab", [(dev, (dev + 1) % 4) for dev in range(4)]))
+    mixed = jnp.roll(
+        jnp.concatenate(ring[::-1], axis=1),
+        (lax.axis_index("vocab") + 1) * ring[0].shape[1],
+        axis=1,
+    )
     mtp_rows = normalize(mixed, mtp_gain).astype(jnp.bfloat16)
     all_rows = jnp.concatenate([main_rows, mtp_rows], axis=0)
     flat_targets = targets.reshape(-1)

time: 927 us -> 907 us (0.978)
  waiting for transfers between devices: 763 us -> 417 us
  starting transfers between devices: 15.1 us -> 290 us
  blocking collectives: 33.8 us -> 100 us
  between operations: 17.9 us -> 4.59 us
    all_gather x1 -> x0, waiting for transfers between devices: 574 us -> none  [shards(): mixed = lax.all_gather(partial_value, 'vocab', axis=1, tiled=True)]
    ppermute x7, starting transfers between devices: 11.6 us -> 286 us  [partner_2(): return lax.ppermute(value, axis, pairs)]
    ppermute x7, waiting for transfers between devices: 188 us -> 400 us  [partner_2(): return lax.ppermute(value, axis, pairs)]
    psum x1, blocking collectives: 22.3 us -> 88 us  [shards(): summed = lax.psum((main_sum, mtp_sum), 'seq')]
    ppermute x0 -> x3, waiting for transfers between devices: none -> 16.7 us  [shards(): lax.ppermute(ring[-1], 'vocab', [(dev, (dev + 1) % 4) for dev in range(4)])]
  transfers between devices with their start and end apart: 9 -> 11, of which waited for: 5 -> 8; matrix products, arithmetic and copies ran while one was open for 8% -> 8% of each run, Pallas kernels for 0% -> 0%
where the time goes in v1:
time: 907 us; the launch traced here: 906 us
  waiting for transfers between devices  417 us (46%)
  starting transfers between devices  290 us (32%)
  blocking collectives  100 us (11%)
  matrix products  50.4 us (6%)
  other arithmetic  38.3 us (4%)
    ppermute x7, waiting for transfers between devices, partner_2(): return lax.ppermute(value, axis, pairs)  400 us
    ppermute x7, starting transfers between devices, partner_2(): return lax.ppermute(value, axis, pairs)  286 us
    psum x1, blocking collectives, shards(): summed = lax.psum((main_sum, mtp_sum), 'seq')  88 us
    dot_general x1, matrix products, shards(): jnp.dot(jnp.concatenate([all_rows, partner], axis=0), held_cols, preferre...  49.2 us
  transfers between devices with their start and end apart: 11, of which 8 were waited for; matrix products, arithmetic and copies ran while one was open for 8% of the time, Pallas kernels for 0%

profile of v1, /device:TPU:0, one launch (start us, length us, event | category | flops | bytes accessed | tf_op | source)
XLA Modules:
  0.0 906.5 jit_solution(5907065701774851470)
XLA Ops:
  0.6 3.1 collective-permute-start.5
  3.7 0.0 copy-start.1
  3.8 0.0 copy-start.2
  3.8 0.0 copy-start.3
  3.8 141.4 %collective-permute-done.5 = bf16[2048,1600]{0,1:T(8,128)(2,1)} collective-permute-done((bf16[2048,1600]{0,1:T(8,128)(2,1)}, bf16[2048,1600]{0,1:T(8,128)(2,1)}, u32[]{:S(2)}, u32[]{:S(2)}) %collective-permute-start.5) | collective-permute-done | bytes 6553632 | tf_op jit(solution)/shard_map/ppermute | solution.py:19
  145.2 15.6 %maximum_select_fusion.2 = bf16[2048,3200]{0,1:T(8,128)(2,1)} fusion(bf16[2048,1600]{0,1:T(8,128)(2,1)} %param.18, bf16[2048,1600]{0,1:T(8,128)(2,1)} %collective-permute-done.5, pred[]{:T(512)S(6)} %eq.43), kind=kLoop, calls=%fused_computation.8 | loop fusion | flops 58982400 | bytes 26214400 | tf_op jit(solution)/shard_map/jit(_where)/select_n | solution.py:98
  160.8 0.0 copy-start.4
  160.8 2.8 collective-permute-start.6
  163.6 0.0 copy-done.1
  163.6 3.4 collective-permute-start
  167.0 0.0 copy-done.2
  167.0 0.3 fusion.15
  167.3 0.0 copy-done.3
  167.3 0.3 fusion.17
  167.6 0.0 copy-start.11
  167.7 0.8 collective-permute-done
  168.4 0.4 multiply_reduce_fusion
  168.9 0.3 maximum_convert_fusion
  169.2 0.0 copy-done.4
  169.2 0.2 fusion.26
  169.5 0.4 copy-done.11
  169.8 0.0 copy-start.5
  169.8 1.2 fusion.27
  171.1 0.0 copy-start.6
  171.1 0.1 collective-permute-start.1
  171.2 5.8 collective-permute-done.1
  176.9 0.0 collective-permute-start.2
  176.9 0.3 fusion.12
  177.3 5.5 collective-permute-done.2
  182.7 0.0 collective-permute-start.3
  182.7 0.0 copy-done.5
  182.7 0.3 fusion.14
  183.1 5.5 collective-permute-done.3
  188.7 0.0 copy-start.7
  188.8 0.3 fusion.18
  189.1 0.0 copy-done.6
  189.1 0.3 fusion.20
  189.4 1.5 pad_maximum_fusion
  190.9 276.9 %collective-permute-start.4 = (bf16[512,2048]{1,0:T(8,128)(2,1)}, bf16[512,2048]{1,0:T(8,128)(2,1)}, u32[]{:S(2)}, u32[]{:S(2)}) collective-permute-start(bf16[512,2048]{1,0:T(8,128)(2,1)} %pad_maximum_fusion), channel_id=1, source_target_pairs={{0,4},{4,0},{8,12},{12,8},{16,20},{20,16},{24,28},{28,24},{1,5},{5... | collective-permute-start | bytes 6291464 | tf_op jit(solution)/shard_map/ppermute | solution.py:19
  467.8 0.0 copy-done.7
  467.8 0.1 collective-permute-start.9
  468.0 45.1 %collective-permute-done.4 = bf16[512,2048]{1,0:T(8,128)(2,1)} collective-permute-done((bf16[512,2048]{1,0:T(8,128)(2,1)}, bf16[512,2048]{1,0:T(8,128)(2,1)}, u32[]{:S(2)}, u32[]{:S(2)}) %collective-permute-start.4) | collective-permute-done | bytes 2097184 | tf_op jit(solution)/shard_map/ppermute | solution.py:19
  513.1 212.6 %collective-permute-done.6 = bf16[2048,3200]{0,1:T(8,128)(2,1)} collective-permute-done((bf16[2048,3200]{0,1:T(8,128)(2,1)}, bf16[2048,3200]{0,1:T(8,128)(2,1)}, u32[]{:S(2)}, u32[]{:S(2)}) %collective-permute-start.6) | collective-permute-done | bytes 13107232 | tf_op jit(solution)/shard_map/ppermute | solution.py:19
  725.7 49.2 %fusion = f32[1024,6400]{1,0:T(8,128)} fusion(bf16[2048,3200]{0,1:T(8,128)(2,1)} %maximum_select_fusion.2, bf16[2048,3200]{0,1:T(8,128)(2,1)} %collective-permute-done.6, pred[]{:T(512)S(6)} %eq.42, bf16[512,2048]{1,0:T(8,128)(2,1)} %collective-permute-done.4, bf16[256,2048]{1,0:T(8,128)(2,1)S(1)} %fusion.20, bf16[256,2048]{1,0:T(8,128)(2,1)S(1)} %bitcast.22), kind=kOutput, calls=%fused_computation.1 | convolution fusion | flops 26974093312 | bytes 56623104 | tf_op jit(solution)/shard_map/dot_general | solution.py:108
  774.8 9.4 %slice_reduce_fusion = (f32[512]{0:T(512)S(1)}, f32[512]{0:T(512)S(1)}) fusion(f32[1024,6400]{1,0:T(8,128)} %fusion), kind=kLoop, calls=%fused_computation.13 | loop fusion | flops 6552576 | bytes 26218496 | tf_op jit(solution)/shard_map/reduce_max | solution.py:29
  784.3 1.4 collective-permute-start.7
  785.7 0.0 collective-permute-done.9
  785.7 5.1 copy-done
  790.8 0.0 copy-start.8
  790.8 0.0 copy-start.9
  790.8 6.9 exponential_reduce_fusion.1
  797.7 1.4 collective-permute-start.10
  799.2 0.0 copy-done.8
  799.2 0.0 copy-done.9
  799.2 0.0 copy-done.10
  799.2 0.8 convert_reduce_fusion
  799.9 0.6 collective-permute-start.8
  800.6 0.0 collective-permute-done.7
  800.6 0.8 collective-permute-done.10
  801.4 5.6 pmax.7
  807.0 0.0 collective-permute-done.8
  807.0 6.6 all-reduce.1
  813.6 1.2 fusion.47
  814.8 88.0 %all-reduce = (f32[]{:T(128)}, f32[]{:T(128)}, f32[]{:T(128)}, f32[]{:T(128)}) all-reduce(f32[]{:T(128)} %get-tuple-element.25, f32[]{:T(128)} %get-tuple-element.27, f32[]{:T(128)} %get-tuple-element.19, f32[]{:T(128)} %get-tuple-element.17), channel_id=1, replica_groups=mesh['seq'=8,'vocab'=4] {'seq'}, use_global_device_ids=true, to_apply=%region_14.15 | all-reduce | flops 4 | bytes 32 | tf_op jit(solution)/shard_map/psum | solution.py:126
  (23 shorter events, 0.3 us)
Async XLA Ops:
  0.6 144.6 %collective-permute-start.5 = (bf16[2048,1600]{0,1:T(8,128)(2,1)}, bf16[2048,1600]{0,1:T(8,128)(2,1)}, u32[]{:S(2)}, u32[]{:S(2)}) collective-permute-start(bf16[2048,1600]{0,1:T(8,128)(2,1)} %param.18), channel_id=1, source_target_pairs={{0,8},{4,12},{8,0},{12,4},{16,24},{20,28},{24,16},{28,20},{1,9},{5... | collective-permute-start | bytes 19660808 | tf_op jit(solution)/shard_map/ppermute | solution.py:19
  3.7 159.8 %copy-start.1 = (bf16[2,128,2048]{2,1,0:T(8,128)(2,1)S(1)}, bf16[2,128,2048]{2,1,0:T(8,128)(2,1)}, u32[]{:S(2)}) copy-start(bf16[2,128,2048]{2,1,0:T(8,128)(2,1)} %param.12) | copy-start | bytes 3145732
  3.8 163.3 %copy-start.2 = (bf16[2,128,2048]{2,1,0:T(8,128)(2,1)S(1)}, bf16[2,128,2048]{2,1,0:T(8,128)(2,1)}, u32[]{:S(2)}) copy-start(bf16[2,128,2048]{2,1,0:T(8,128)(2,1)} %param.13) | copy-start | bytes 3145732
  3.8 163.6 %copy-start.3 = (f32[2048]{0:T(1024)S(1)}, f32[2048]{0:T(1024)}, u32[]{:S(2)}) copy-start(f32[2048]{0:T(1024)} %param.22) | copy-start | bytes 24580
  160.8 8.4 copy-start.4
  160.8 564.8 %collective-permute-start.6 = (bf16[2048,3200]{0,1:T(8,128)(2,1)}, bf16[2048,3200]{0,1:T(8,128)(2,1)}, u32[]{:S(2)}, u32[]{:S(2)}) collective-permute-start(bf16[2048,3200]{0,1:T(8,128)(2,1)} %maximum_select_fusion.2), channel_id=1, source_target_pairs={{0,16},{4,20},{8,24},{12,28},{16,0},{20,4},{24,8},{28,12},{1,17},{... | collective-permute-start | bytes 39321608 | tf_op jit(solution)/shard_map/ppermute | solution.py:19
  163.6 4.8 collective-permute-start
  167.6 2.2 copy-start.11
  169.8 12.9 %copy-start.5 = (f32[2048]{0:T(1024)S(1)}, f32[2048]{0:T(1024)}, u32[]{:S(2)}) copy-start(f32[2048]{0:T(1024)} %param.20) | copy-start | bytes 24580
  171.1 18.0 %copy-start.6 = (f32[2048]{0:T(1024)S(1)}, f32[2048]{0:T(1024)}, u32[]{:S(2)}) copy-start(f32[2048]{0:T(1024)} %param.23) | copy-start | bytes 24580
  171.1 5.8 collective-permute-start.1
  176.9 5.8 collective-permute-start.2
  182.7 5.8 collective-permute-start.3
  188.7 279.1 %copy-start.7 = (s32[2,128]{1,0:T(2,128)S(1)}, s32[2,128]{1,0:T(2,128)}, u32[]{:S(2)}) copy-start(s32[2,128]{1,0:T(2,128)} %param.14) | copy-start | bytes 3076
  190.9 322.2 %collective-permute-start.4 = (bf16[512,2048]{1,0:T(8,128)(2,1)}, bf16[512,2048]{1,0:T(8,128)(2,1)}, u32[]{:S(2)}, u32[]{:S(2)}) collective-permute-start(bf16[512,2048]{1,0:T(8,128)(2,1)} %pad_maximum_fusion), channel_id=1, source_target_pairs={{0,4},{4,0},{8,12},{12,8},{16,20},{20,16},{24,28},{28,24},{1,5},{5... | collective-permute-start | bytes 6291464 | tf_op jit(solution)/shard_map/ppermute | solution.py:19
  467.8 317.9 %collective-permute-start.9 = (s32[512]{0:T(512)S(1)}, s32[512]{0:T(512)S(1)}, u32[]{:S(2)}, u32[]{:S(2)}) collective-permute-start(s32[512]{0:T(512)S(1)} %pad_add_fusion), channel_id=1, source_target_pairs={{0,4},{4,0},{8,12},{12,8},{16,20},{20,16},{24,28},{28,24},{1,5},{5... | collective-permute-start | bytes 6152 | tf_op jit(solution)/shard_map/ppermute | solution.py:19
  774.8 16.0 %copy-start = (f32[1024,6400]{1,0:T(8,128)S(1)}, f32[1024,6400]{1,0:T(8,128)}, u32[]{:S(2)}) copy-start(f32[1024,6400]{1,0:T(8,128)} %fusion) | copy-start | bytes 78643200
  784.3 16.3 %collective-permute-start.7 = (f32[512]{0:T(512)S(1)}, f32[512]{0:T(512)S(1)}, u32[]{:S(2)}, u32[]{:S(2)}) collective-permute-start(f32[512]{0:T(512)S(1)} %get-tuple-element.9), channel_id=1, source_target_pairs={{0,4},{4,0},{8,12},{12,8},{16,20},{20,16},{24,28},{28,24},{1,5},{5... | collective-permute-start | bytes 6152 | tf_op jit(solution)/shard_map/ppermute | solution.py:19
  790.8 8.4 copy-start.8
  790.8 8.4 copy-start.9
  790.8 8.4 copy-start.10
  797.7 3.6 collective-permute-start.10
  799.9 7.1 collective-permute-start.8
